TPU v7x, 32 devices: a whole 2x2x4 slice. The times are simulated.
32 devices in a mesh: dp: 8 (over y, x, core), tensor: 4 (over z).
Axes of the slice: x: 2, y: 2, z: 4, core: 2. Of those that a mesh axis runs over, the one named last changes fastest.
Arguments:
- enc_hidden: bfloat16 [16384, 4096], P(('dp', 'tensor')), parts along dimension 0, may hold values from -6 to 6
- enc_gain: float32 [4096], replicated, may hold values from 0.1 to 1.9
- dec_hidden: bfloat16 [4096, 4096], P(('dp', 'tensor')), parts along dimension 0, may hold values from -6 to 6
- dec_gain: float32 [4096], replicated, may hold values from 0.8 to 12, as said below
- w_query: bfloat16 [4096, 4096], P(None, 'tensor'), may hold values from -0.046875 to 0.046875
- w_key: bfloat16 [4096, 4096], P(None, 'tensor'), may hold values from -0.09375 to 0.09375
- w_value: bfloat16 [4096, 4096], P(None, 'tensor'), may hold values from -0.09375 to 0.09375
- w_out: bfloat16 [4096, 4096], P('tensor'), may hold values from -0.75 to 0.75
- enc_length: int32 [8], P('dp'), parts along dimension 0, may hold values from 1024 to 2048
- dec_length: int32 [8], P('dp'), parts along dimension 0, may hold values from 256 to 512
Outputs:
- memory: bfloat16 [16384, 4096], P(('dp', 'tensor')), parts along dimension 0
- cross_out: bfloat16 [4096, 4096], P(('dp', 'tensor')), parts along dimension 0
There are 8 independent parts, one for each index of `dp`. A program takes and returns all parts, laid end to end along the dimension named above; an argument that names none is the same for every part. Nothing has to cross between parts.
Inputs may be any that keep to these rules, and one draw needn't show every extreme that they name: `dec_gain`: positive.
All inputs are finite; a program needn't handle non-finite values.
Results may differ from a plain program's by a relative error of at most 0.02.
The roundings to bfloat16 on the way count: a program that leaves them out, or rounds other values in their place, can miss the bound.
Values may be sent and summed in bfloat16 or wider, within the bound.
No kernel may reach another device: no remote copies, remote signals or barrier semaphores. Data moves between devices by JAX's collectives and lax.ppermute only.
A program may use at most 192 MiB of HBM per device.

v0:
```python
import jax
import jax.numpy as jnp
from jax import lax
from jax.sharding import PartitionSpec as P

HEAD_DIM = 64
ENC_LEN = 2048
DEC_LEN = 512


def rms_norm(values, gain):
    wide = values.astype(jnp.float32)
    mean_sq = jnp.mean(wide * wide, axis=-1, keepdims=True)
    return (wide * lax.rsqrt(mean_sq + 1e-06) * gain).astype(jnp.bfloat16)


def shards(
    enc_hidden,
    enc_gain,
    dec_hidden,
    dec_gain,
    w_query,
    w_key,
    w_value,
    w_out,
    enc_length,
    dec_length,
):
    memory = rms_norm(enc_hidden, enc_gain)
    normed = rms_norm(dec_hidden, dec_gain)
    local_width = w_query.shape[1]
    local_heads = local_width // HEAD_DIM
    dec_rows = dec_hidden.shape[0]
    all_normed = lax.all_gather(normed, "tensor", axis=0, tiled=True)
    queries = jnp.dot(all_normed, w_query, preferred_element_type=jnp.float32).astype(jnp.bfloat16)
    q_heads = queries.reshape(DEC_LEN, local_heads, HEAD_DIM)
    segment = lax.all_gather(memory, "tensor", axis=0, tiled=True)
    key_part = jnp.dot(segment, w_key, preferred_element_type=jnp.float32).astype(jnp.bfloat16)
    value_part = jnp.dot(segment, w_value, preferred_element_type=jnp.float32).astype(jnp.bfloat16)
    paired = jnp.concatenate([key_part, value_part], axis=1)
    key_rows = paired[:, :local_width]
    value_rows = paired[:, local_width:]
    k_heads = key_rows.reshape(ENC_LEN, local_heads, HEAD_DIM)
    scores = jnp.einsum("qhd,khd->hqk", q_heads, k_heads, preferred_element_type=jnp.float32)
    valid_keys = jnp.arange(ENC_LEN, dtype=jnp.int32) < enc_length[0]
    scores = jnp.where(valid_keys[None, None, :], scores, -jnp.inf)
    weights = jax.nn.softmax(scores, axis=-1).astype(jnp.bfloat16)
    v_heads = value_rows.reshape(ENC_LEN, local_heads, HEAD_DIM)
    context = jnp.einsum("hqk,khd->qhd", weights, v_heads, preferred_element_type=jnp.float32)
    context = context.astype(jnp.bfloat16).reshape(DEC_LEN, local_width)
    projected = lax.psum_scatter(
        jnp.dot(context, w_out, preferred_element_type=jnp.float32).astype(jnp.bfloat16),
        "tensor",
        scatter_dimension=0,
        tiled=True,
    ).astype(jnp.float32)
    row_ids = lax.axis_index("tensor") * dec_rows + jnp.arange(dec_rows, dtype=jnp.int32)
    live_rows = row_ids < dec_length[0]
    cross_out = jnp.where(live_rows[:, None], projected, 0.0).astype(jnp.bfloat16)
    return (memory, cross_out)


def solution(mesh):
    placed = (
        P(("dp", "tensor"), None),
        P(),
        P(("dp", "tensor"), None),
        P(),
        P(None, "tensor"),
        P(None, "tensor"),
        P(None, "tensor"),
        P("tensor", None),
        P("dp"),
        P("dp"),
    )
    return jax.shard_map(
        shards,
        mesh=mesh,
        in_specs=placed,
        out_specs=(P(("dp", "tensor"), None), P(("dp", "tensor"), None)),
        check_vma=False,
    )
```

profile of v0, /device:TPU:0, one launch (start us, length us, event | category | flops | bytes accessed | tf_op | source)
XLA Modules:
  0.0 576.0 jit_solution(13626997619669954659)
XLA Ops:
  7.2 0.0 copy-start
  7.2 0.0 all-gather.5.cloned.1.call-start
  7.2 1.5 fusion.10
  8.7 2.5 fusion.12
  11.3 0.0 all-gather.5.cloned.1.call-update
  11.3 0.0 all-gather.3.cloned.1.call-start
  11.4 3.1 fusion.7
  14.4 0.0 copy-done
  14.5 5.8 %fusion.9 = bf16[512,4096]{1,0:T(8,128)(2,1)} fusion(bf16[512,4096]{1,0:T(8,128)(2,1)} %param.10, f32[4096]{0:T(1024)S(1)} %copy-done, f32[512]{0:T(512)S(1)} %add_rsqrt_fusion), kind=kLoop, calls=%fused_computation.12 | loop fusion | flops 8388608 | bytes 8407040 | tf_op jit(solution)/shard_map/convert_element_type | solution.py:14
  20.3 0.0 all-gather.3.cloned.1.call-update
  20.3 0.0 reduce-scatter.2.cloned.1.call-start
  21.0 73.9 %all-gather.5.cloned.1.call-done = bf16[512,4096]{1,0:T(8,128)(2,1)} async-done(((bf16[128,4096]{1,0:T(8,128)(2,1)}), bf16[512,4096]{1,0:T(8,128)(2,1)}) %all-gather.5.cloned.1.call-update) | async-done | bytes 4194320 | tf_op jit(solution)/shard_map/all_gather | solution.py:34
  94.9 9.1 %convolution_convert_fusion.3 = bf16[512,1024]{1,0:T(8,128)(2,1)S(1)} fusion(bf16[512,4096]{1,0:T(8,128)(2,1)} %all-gather.5.cloned.1.call-done, bf16[4096,1024]{1,0:T(8,128)(2,1)} %param.14), kind=kOutput, calls=%fused_computation.22 | convolution fusion | flops 4295491584 | bytes 13631488 | tf_op jit(solution)/shard_map/dot_general | solution.py:35
  104.1 0.7 copy.13
  104.8 277.5 %all-gather.3.cloned.1.call-done = bf16[2048,4096]{1,0:T(8,128)(2,1)} async-done(((bf16[512,4096]{1,0:T(8,128)(2,1)}), bf16[2048,4096]{1,0:T(8,128)(2,1)}) %all-gather.3.cloned.1.call-update) | async-done | bytes 16777232 | tf_op jit(solution)/shard_map/all_gather | solution.py:37
  382.3 23.9 %convolution_convert_fusion.1 = bf16[2048,1024]{0,1:T(8,128)(2,1)} fusion(bf16[2048,4096]{1,0:T(8,128)(2,1)} %all-gather.3.cloned.1.call-done, bf16[4096,1024]{1,0:T(8,128)(2,1)} %param.15), kind=kOutput, calls=%fused_computation.14 | convolution fusion | flops 17181966336 | bytes 29360128 | tf_op jit(solution)/shard_map/dot_general | solution.py:38
  406.2 27.6 %fusion.17 = (f32[16,512]{1,0:T(8,128)S(1)}, f32[16,512,2048]{2,1,0:T(8,128)}) fusion(pred[2048]{0:T(1024)(128)(4,1)S(1)} %iota_compare_fusion, bf16[512,16,64]{0,2,1:T(8,128)(2,1)S(1)} %bitcast.23, bf16[2048,16,64]{0,2,1:T(8,128)(2,1)} %bitcast.24), kind=kOutput, calls=%fused_computation.30 | convolution fusion | flops 2197817344 | bytes 72386560 | tf_op jit(solution)/shard_map/sub | solution.py:47
  433.8 23.9 %convolution_convert_fusion.2 = bf16[2048,1024]{0,1:T(8,128)(2,1)} fusion(bf16[2048,4096]{1,0:T(8,128)(2,1)} %all-gather.3.cloned.1.call-done, bf16[4096,1024]{1,0:T(8,128)(2,1)} %param.16), kind=kOutput, calls=%fused_computation.15 | convolution fusion | flops 17181966336 | bytes 29360128 | tf_op jit(solution)/shard_map/dot_general | solution.py:39
  457.7 24.7 %fusion.13 = bf16[16,64,512]{2,1,0:T(8,128)(2,1)S(1)} fusion(bf16[2048,16,64]{0,2,1:T(8,128)(2,1)} %bitcast.25, f32[16,512,2048]{2,1,0:T(8,128)} %get-tuple-element.3, f32[16,512]{1,0:T(8,128)S(1)} %get-tuple-element.2), kind=kOutput, calls=%fused_computation.23 | convolution fusion | flops 2181562368 | bytes 72384512 | tf_op jit(solution)/shard_map/hqk,khd->qhd/dot_general | solution.py:49
  482.4 9.5 %convolution_convert_fusion = bf16[512,4096]{1,0:T(8,128)(2,1)} fusion(bf16[512,1024]{0,1:T(8,128)(2,1)S(1)} %bitcast.26, bf16[1024,4096]{1,0:T(8,128)(2,1)} %param.17), kind=kOutput, calls=%fused_computation.13 | convolution fusion | flops 4297064448 | bytes 13631488 | tf_op jit(solution)/shard_map/dot_general | solution.py:52
  491.9 0.0 reduce-scatter.2.cloned.1.call-update
  492.6 74.5 %reduce-scatter.2.cloned.1.call-done = bf16[128,4096]{1,0:T(8,128)(2,1)} async-done(((bf16[512,4096]{1,0:T(8,128)(2,1)}), bf16[128,4096]{1,0:T(8,128)(2,1)}) %reduce-scatter.2.cloned.1.call-update) | async-done | bytes 1048592 | tf_op jit(solution)/shard_map/reduce_scatter | solution.py:51
  567.0 2.5 select_convert_fusion
  (4 shorter events, 0.0 us)
Async XLA Ops:
  7.2 7.3 %copy-start = (f32[4096]{0:T(1024)S(1)}, f32[4096]{0:T(1024)}, u32[]{:S(2)}) copy-start(f32[4096]{0:T(1024)} %param.11) | copy-start | bytes 49156
  7.2 87.7 %all-gather.5.cloned.1.call-start = ((), (), s32[]{:S(2)}) async-start(), calls=%async_computation.2 | async-start | bytes 5242880 | tf_op jit(solution)/shard_map/all_gather | solution.py:34
  11.3 371.0 %all-gather.3.cloned.1.call-start = ((), (), s32[]{:S(2)}) async-start(), calls=%async_computation.1 | async-start | bytes 20971520 | tf_op jit(solution)/shard_map/all_gather | solution.py:37
  20.3 546.7 %reduce-scatter.2.cloned.1.call-start = ((), (), s32[]{:S(2)}) async-start(), calls=%async_computation.3 | async-start | bytes 5242880 | tf_op jit(solution)/shard_map/reduce_scatter | solution.py:51
Sparse Core Ops, SparseCore 0:
  11.4 83.4 all-gather.4
  97.1 285.2 all-gather.2
  492.0 74.9 reduce-scatter.1
where the time goes:
time: 576 us
  waiting for transfers between devices  426 us (74%)
  matrix products  119 us (21%)
  other arithmetic  15.5 us (3%)
  between operations  15.1 us (3%)
    all_gather x1, waiting for transfers between devices, shards(): segment = lax.all_gather(memory, 'tensor', axis=0, tiled=True)  278 us
    reduce_scatter x1, waiting for transfers between devices, shards(): lax.psum_scatter(jnp.dot(context, w_out, preferred_element_type=jnp.float...  74.5 us
    all_gather x1, waiting for transfers between devices, shards(): all_normed = lax.all_gather(normed, 'tensor', axis=0, tiled=True)  73.9 us
    sub x1, matrix products, shards(): weights = jax.nn.softmax(scores, axis=-1).astype(jnp.bfloat16)  27.6 us
    dot_general x1, matrix products, shards(): jnp.einsum('hqk,khd->qhd', weights, v_heads, preferred_element_type=jnp.f...  24.7 us
    dot_general x1, matrix products, shards(): jnp.dot(segment, w_key, preferred_element_type=jnp.float32)  23.9 us
    dot_general x1, matrix products, shards(): jnp.dot(segment, w_value, preferred_element_type=jnp.float32)  23.9 us
  transfers between devices with their start and end apart: 3, of which 3 were waited for; matrix products, arithmetic and copies ran while one was open for 3% of the time, Pallas kernels for 0%

commit v1 on v0

--- a/solution.py
+++ b/solution.py
@@ -6,6 +6,28 @@
 HEAD_DIM = 64
 ENC_LEN = 2048
 DEC_LEN = 512
+
+
+def laid_out(parts, dim):
+    shape = list(parts.shape[1:])
+    shape[dim] *= parts.shape[0]
+    return jnp.moveaxis(parts, 0, dim).reshape(shape)
+
+
+def ring_gather(x, axis, dim):
+    size = lax.axis_size(axis)
+    pairs = [(i, (i + 1) % size) for i in range(size)]
+    back = [(b, a) for a, b in pairs]
+    lower, upper = ([], [])
+    for step in range(size - 1):
+        if step % 2 == 0:
+            lower.append(lax.ppermute(lower[-1] if lower else x, axis, pairs))
+        else:
+            upper.append(lax.ppermute(upper[-1] if upper else x, axis, back))
+    blocks = jnp.stack([*lower[::-1], x, *upper])
+    shift = lax.axis_index(axis) - len(lower)
+    blocks = blocks[(jnp.arange(size) - shift) % size]
+    return laid_out(blocks, dim)
 
 
 def rms_norm(values, gain):
@@ -31,7 +53,7 @@
     local_width = w_query.shape[1]
     local_heads = local_width // HEAD_DIM
     dec_rows = dec_hidden.shape[0]
-    all_normed = lax.all_gather(normed, "tensor", axis=0, tiled=True)
+    all_normed = ring_gather(normed, "tensor", 0)
     queries = jnp.dot(all_normed, w_query, preferred_element_type=jnp.float32).astype(jnp.bfloat16)
     q_heads = queries.reshape(DEC_LEN, local_heads, HEAD_DIM)
     segment = lax.all_gather(memory, "tensor", axis=0, tiled=True)

time: 576 us -> 556 us (0.965)
  waiting for transfers between devices: 426 us -> 352 us
  starting transfers between devices: 0.12 us -> 47.8 us
  local copies, waits for them, and re-layouts: 0.73 us -> 6.9 us
    all_gather x1, waiting for transfers between devices: 278 us -> 196 us  [shards(): segment = lax.all_gather(memory, 'tensor', axis=0, tiled=True)]
    ppermute x0 -> x3, waiting for transfers between devices: none -> 81.3 us  [the longest x2 60.3 us: ring_gather(): lower.append(lax.ppermute(lower[-1] if lower else x, axis, pairs))]
    all_gather x1 -> x0, waiting for transfers between devices: 73.9 us -> none  [shards(): all_normed = lax.all_gather(normed, 'tensor', axis=0, tiled=True)]
    ppermute x0 -> x3, starting transfers between devices: none -> 47.7 us  [the longest x2 45.6 us: ring_gather(): lower.append(lax.ppermute(lower[-1] if lower else x, axis, pairs))]
  transfers between devices with their start and end apart: 3 -> 5, of which waited for: 3 -> 5; matrix products, arithmetic and copies ran while one was open for 3% -> 3% of each run, Pallas kernels for 0% -> 0%
where the time goes in v1:
time: 556 us
  waiting for transfers between devices  352 us (63%)
  matrix products  119 us (21%)
  starting transfers between devices  47.8 us (9%)
  between operations  15.4 us (3%)
  other arithmetic  14.3 us (3%)
  local copies, waits for them, and re-layouts  6.9 us (1%)
    all_gather x1, waiting for transfers between devices, shards(): segment = lax.all_gather(memory, 'tensor', axis=0, tiled=True)  196 us
    reduce_scatter x1, waiting for transfers between devices, shards(): lax.psum_scatter(jnp.dot(context, w_out, preferred_element_type=jnp.float...  75.5 us
    ppermute x2, waiting for transfers between devices, ring_gather(): lower.append(lax.ppermute(lower[-1] if lower else x, axis, pairs))  60.3 us
    ppermute x2, starting transfers between devices, ring_gather(): lower.append(lax.ppermute(lower[-1] if lower else x, axis, pairs))  45.6 us
    sub x1, matrix products, shards(): weights = jax.nn.softmax(scores, axis=-1).astype(jnp.bfloat16)  27.5 us
    dot_general x1, matrix products, shards(): jnp.einsum('hqk,khd->qhd', weights, v_heads, preferred_element_type=jnp.f...  24.7 us
    dot_general x1, matrix products, shards(): jnp.dot(segment, w_key, preferred_element_type=jnp.float32)  23.9 us
    dot_general x1, matrix products, shards(): jnp.dot(segment, w_value, preferred_element_type=jnp.float32)  23.9 us
  transfers between devices with their start and end apart: 5, of which 5 were waited for; matrix products, arithmetic and copies ran while one was open for 3% of the time, Pallas kernels for 0%

profile of v1, /device:TPU:0, one launch (start us, length us, event | category | flops | bytes accessed | tf_op | source)
XLA Modules:
  0.0 555.7 jit_solution(11714157248687442645)
XLA Ops:
  7.2 3.2 fusion.7
  10.7 4.4 fusion.9
  15.1 1.1 copy-done.1
  16.2 0.3 fusion.10
  16.5 0.3 fusion.12
  16.9 3.1 collective-permute-start
  20.0 2.1 collective-permute-start.2
  22.8 35.1 %collective-permute-done = bf16[128,4096]{1,0:T(8,128)(2,1)S(1)} collective-permute-done((bf16[128,4096]{1,0:T(8,128)(2,1)S(1)}, bf16[128,4096]{1,0:T(8,128)(2,1)S(1)}, u32[]{:S(2)}, u32[]{:S(2)}) %collective-permute-start) | collective-permute-done | bytes 1048608 | tf_op jit(solution)/shard_map/ppermute | solution.py:24
  57.8 42.5 %collective-permute-start.1 = (bf16[128,4096]{1,0:T(8,128)(2,1)S(1)}, bf16[128,4096]{1,0:T(8,128)(2,1)S(1)}, u32[]{:S(2)}, u32[]{:S(2)}) collective-permute-start(bf16[128,4096]{1,0:T(8,128)(2,1)S(1)} %collective-permute-done), channel_id=1, source_target_pairs={{0,1},{1,2},{2,3},{3,0},{4,5},{5,6},{6,7},{7,4},{8,9},{9,10},{10,1... | collective-permute-start | bytes 3145736 | tf_op jit(solution)/shard_map/ppermute | solution.py:24
  100.4 0.3 fusion.33
  100.7 21.0 %collective-permute-done.2 = bf16[128,4096]{1,0:T(8,128)(2,1)} collective-permute-done((bf16[128,4096]{1,0:T(8,128)(2,1)S(1)}, bf16[128,4096]{1,0:T(8,128)(2,1)}, u32[]{:S(2)}, u32[]{:S(2)}) %collective-permute-start.2) | collective-permute-done | bytes 1048608 | tf_op jit(solution)/shard_map/ppermute | solution.py:26
  121.7 25.2 %collective-permute-done.1 = bf16[128,4096]{1,0:T(8,128)(2,1)S(1)} collective-permute-done((bf16[128,4096]{1,0:T(8,128)(2,1)S(1)}, bf16[128,4096]{1,0:T(8,128)(2,1)S(1)}, u32[]{:S(2)}, u32[]{:S(2)}) %collective-permute-start.1) | collective-permute-done | bytes 1048608 | tf_op jit(solution)/shard_map/ppermute | solution.py:24
  146.9 3.3 pad_maximum_fusion
  150.2 5.0 gather_fusion
  155.2 9.2 %convolution_convert_fusion.3 = bf16[512,1024]{1,0:T(8,128)(2,1)S(1)} fusion(bf16[512,4096]{1,0:T(8,128)(2,1)} %bitcast.31, bf16[4096,1024]{1,0:T(8,128)(2,1)} %param.14), kind=kOutput, calls=%fused_computation.24 | convolution fusion | flops 4295491584 | bytes 13631488 | tf_op jit(solution)/shard_map/dot_general | solution.py:57
  164.4 0.5 copy.13
  164.9 195.5 %all-gather.2.cloned.1.call-done = bf16[2048,4096]{1,0:T(8,128)(2,1)} async-done(((bf16[512,4096]{1,0:T(8,128)(2,1)}), bf16[2048,4096]{1,0:T(8,128)(2,1)}) %all-gather.2.cloned.1.call-update) | async-done | bytes 16777232 | tf_op jit(solution)/shard_map/all_gather | solution.py:59
  360.4 23.9 %convolution_convert_fusion.1 = bf16[2048,1024]{0,1:T(8,128)(2,1)} fusion(bf16[2048,4096]{1,0:T(8,128)(2,1)} %all-gather.2.cloned.1.call-done, bf16[4096,1024]{1,0:T(8,128)(2,1)} %param.15), kind=kOutput, calls=%fused_computation.16 | convolution fusion | flops 17181966336 | bytes 29360128 | tf_op jit(solution)/shard_map/dot_general | solution.py:60
  384.3 27.5 %fusion.19 = (f32[16,512]{1,0:T(8,128)S(1)}, f32[16,512,2048]{2,1,0:T(8,128)}) fusion(pred[2048]{0:T(1024)(128)(4,1)S(1)} %iota_compare_fusion, bf16[512,16,64]{0,2,1:T(8,128)(2,1)S(1)} %bitcast.32, bf16[2048,16,64]{0,2,1:T(8,128)(2,1)} %bitcast.35), kind=kOutput, calls=%fused_computation.39 | convolution fusion | flops 2197817344 | bytes 72386560 | tf_op jit(solution)/shard_map/sub | solution.py:69
  411.9 23.9 %convolution_convert_fusion.2 = bf16[2048,1024]{0,1:T(8,128)(2,1)} fusion(bf16[2048,4096]{1,0:T(8,128)(2,1)} %all-gather.2.cloned.1.call-done, bf16[4096,1024]{1,0:T(8,128)(2,1)} %param.16), kind=kOutput, calls=%fused_computation.17 | convolution fusion | flops 17181966336 | bytes 29360128 | tf_op jit(solution)/shard_map/dot_general | solution.py:61
  435.7 24.7 %fusion.13 = bf16[16,64,512]{2,1,0:T(8,128)(2,1)S(1)} fusion(bf16[2048,16,64]{0,2,1:T(8,128)(2,1)} %bitcast.36, f32[16,512,2048]{2,1,0:T(8,128)} %get-tuple-element.3, f32[16,512]{1,0:T(8,128)S(1)} %get-tuple-element.2), kind=kOutput, calls=%fused_computation.25 | convolution fusion | flops 2181562368 | bytes 72384512 | tf_op jit(solution)/shard_map/hqk,khd->qhd/dot_general | solution.py:71
  460.5 9.7 %convolution_convert_fusion = bf16[512,4096]{1,0:T(8,128)(2,1)} fusion(bf16[512,1024]{0,1:T(8,128)(2,1)S(1)} %bitcast.37, bf16[1024,4096]{1,0:T(8,128)(2,1)} %param.17), kind=kOutput, calls=%fused_computation.14 | convolution fusion | flops 4297064448 | bytes 13631488 | tf_op jit(solution)/shard_map/dot_general | solution.py:74
  470.9 75.5 %reduce-scatter.2.cloned.1.call-done = bf16[128,4096]{1,0:T(8,128)(2,1)} async-done(((bf16[512,4096]{1,0:T(8,128)(2,1)}), bf16[128,4096]{1,0:T(8,128)(2,1)}) %reduce-scatter.2.cloned.1.call-update) | async-done | bytes 1048592 | tf_op jit(solution)/shard_map/reduce_scatter | solution.py:73
  546.4 2.5 select_convert_fusion
  (15 shorter events, 0.4 us)
Async XLA Ops:
  7.2 353.3 %all-gather.2.cloned.1.call-start = ((), (), s32[]{:S(2)}) async-start(), calls=%async_computation.1 | async-start | bytes 20971520 | tf_op jit(solution)/shard_map/all_gather | solution.py:59
  7.2 3.5 copy-start
  15.0 1.2 copy-start.1
  15.0 1.5 copy-start.2
  15.0 531.4 %reduce-scatter.2.cloned.1.call-start = ((), (), s32[]{:S(2)}) async-start(), calls=%async_computation.2 | async-start | bytes 5242880 | tf_op jit(solution)/shard_map/reduce_scatter | solution.py:73
  16.9 41.0 %collective-permute-start = (bf16[128,4096]{1,0:T(8,128)(2,1)S(1)}, bf16[128,4096]{1,0:T(8,128)(2,1)S(1)}, u32[]{:S(2)}, u32[]{:S(2)}) collective-permute-start(bf16[128,4096]{1,0:T(8,128)(2,1)S(1)} %fusion.12), channel_id=1, source_target_pairs={{0,1},{1,2},{2,3},{3,0},{4,5},{5,6},{6,7},{7,4},{8,9},{9,10},{10,1... | collective-permute-start | bytes 3145736 | tf_op jit(solution)/shard_map/ppermute | solution.py:24
  20.0 101.7 %collective-permute-start.2 = (bf16[128,4096]{1,0:T(8,128)(2,1)S(1)}, bf16[128,4096]{1,0:T(8,128)(2,1)}, u32[]{:S(2)}, u32[]{:S(2)}) collective-permute-start(bf16[128,4096]{1,0:T(8,128)(2,1)S(1)} %fusion.12), channel_id=1, source_target_pairs={{1,0},{2,1},{3,2},{0,3},{5,4},{6,5},{7,6},{4,7},{9,8},{10,9},{11,1... | collective-permute-start | bytes 3145736 | tf_op jit(solution)/shard_map/ppermute | solution.py:26
  57.8 89.0 %collective-permute-start.1 = (bf16[128,4096]{1,0:T(8,128)(2,1)S(1)}, bf16[128,4096]{1,0:T(8,128)(2,1)S(1)}, u32[]{:S(2)}, u32[]{:S(2)}) collective-permute-start(bf16[128,4096]{1,0:T(8,128)(2,1)S(1)} %collective-permute-done), channel_id=1, source_target_pairs={{0,1},{1,2},{2,3},{3,0},{4,5},{5,6},{6,7},{7,4},{8,9},{9,10},{10,1... | collective-permute-start | bytes 3145736 | tf_op jit(solution)/shard_map/ppermute | solution.py:24
Sparse Core Ops, SparseCore 0:
  15.2 345.2 all-gather.1
  470.3 76.0 reduce-scatter.1
